TPU v7x, 256 devices: a whole 4x4x8 slice. The times are simulated.
256 devices in a mesh: row: 8 (over z_hi, core), col: 32 (over z_lo, x, y).
Axes of the slice: x: 4, y: 4, z: 8 (z_hi: 4, z_lo: 2; z = z_hi * 2 + z_lo), core: 2. Of those that a mesh axis runs over, the one named last changes fastest.
Arguments:
- panel_adj: float32 [14336, 512], P('row', 'col'), may hold values from -6 to 6
- inv_diag: float32 [512, 512], P('col'), may hold values from -0.25 to 0.25
- row_panel: float32 [512, 14336], P('row', 'col'), may hold values from -0.25 to 0.25
- trailing_adj: float32 [14336, 14336], P('row', 'col'), may hold values from -6 to 6
- trailing_factor: float32 [14336, 14336], P('row', 'col'), may hold values from -0.046875 to 0.046875
Outputs:
- trailing_new: float32 [14336, 14336], P('row', 'col')
- row_adj: float32 [512, 14336], P('row', 'col')
All inputs are finite; a program needn't handle non-finite values.
Results may differ from a plain program's by a relative error of at most 0.00007.
Values sent between devices are 32-bit elements; how exact they have to be, the bound alone decides.
A program may use at most 64 MiB of HBM per device.

v0:
```python
import jax
import jax.numpy as jnp
from jax import lax
from jax.sharding import PartitionSpec as P


def local(panel_adj, inv_diag, row_panel, trailing_adj, trailing_factor):
    highest = lax.Precision.HIGHEST
    inverse_all = lax.all_gather(inv_diag, "col", axis=0, tiled=True)
    scaled = jnp.dot(
        lax.all_gather(panel_adj, "col", axis=1, tiled=True),
        inverse_all,
        precision=highest,
        preferred_element_type=jnp.float32,
    )
    trailing_new = trailing_adj - jnp.dot(
        scaled,
        lax.all_gather(row_panel, "row", axis=0, tiled=True),
        precision=highest,
        preferred_element_type=jnp.float32,
    )
    terms_local = lax.dot_general(
        scaled,
        trailing_factor,
        (((0,), (0,)), ((), ())),
        precision=highest,
        preferred_element_type=jnp.float32,
    )
    row_adj = lax.psum_scatter(terms_local, "row", scatter_dimension=0, tiled=True)
    return (trailing_new, row_adj)


def solution(mesh):
    placed = (P("row", "col"), P("col", None), P("row", "col"), P("row", "col"), P("row", "col"))
    return jax.shard_map(
        local,
        mesh=mesh,
        in_specs=placed,
        out_specs=(P("row", "col"), P("row", "col")),
        check_vma=False,
    )
```

profile of v0, /device:TPU:1, one launch (start us, length us, event | category | flops | bytes accessed | tf_op | source)
XLA Modules:
  0.0 396.5 jit_solution(17460314961301271969)
XLA Ops:
  7.2 0.0 copy-start
  7.2 0.0 all-gather.5.cloned.1.call-start
  7.2 0.7 all-gather.5.cloned.1.call-update
  7.9 0.0 all-gather.3.cloned.1.call-start
  8.0 0.7 all-gather.3.cloned.1.call-update
  8.7 0.0 reduce-scatter.2.cloned.1.call-start
  8.7 135.8 %all-gather.5.cloned.1.call-done = f32[512,512]{1,0:T(8,128)} async-done(((f32[16,512]{1,0:T(8,128)}), f32[512,512]{1,0:T(8,128)}) %all-gather.5.cloned.1.call-update) | async-done | bytes 1048592 | tf_op jit(solution)/shard_map/all_gather | solution.py:9
  144.6 161.2 %all-gather.3.cloned.1.call-done = f32[1792,512]{0,1:T(8,128)} async-done(((f32[1792,16]{0,1:T(8,128)}), f32[1792,512]{0,1:T(8,128)}) %all-gather.3.cloned.1.call-update) | async-done | bytes 3670032 | tf_op jit(solution)/shard_map/all_gather | solution.py:11
  305.7 8.5 %fusion = f32[1792,512]{1,0:T(8,128)S(1)} fusion(f32[1792,512]{0,1:T(8,128)} %all-gather.3.cloned.1.call-done, f32[512,512]{1,0:T(8,128)} %all-gather.5.cloned.1.call-done), kind=kOutput, calls=%fused_computation.1 | convolution fusion | flops 5637144576 | bytes 8388608 | tf_op jit(solution)/shard_map/dot_general | solution.py:10
  314.3 0.0 copy-start.1
  314.3 1.8 copy-done.1
  316.1 0.0 copy-done
  316.1 0.0 copy-start.2
  316.1 13.0 %fusion.1 = f32[512,448]{1,0:T(8,128)} fusion(f32[1792,512]{1,0:T(8,128)S(1)} %fusion, f32[1792,448]{0,1:T(8,128)S(1)} %copy-done), kind=kOutput, calls=%fused_computation.2 | convolution fusion | flops 4932501504 | bytes 7798784 | tf_op jit(solution)/shard_map/dot_general | solution.py:22
  329.1 0.0 reduce-scatter.2.cloned.1.call-update
  329.1 0.0 copy-done.2
  329.1 42.0 %all_gather.11 = f32[512,448]{1,0:T(8,128)S(1)} all-gather(f32[64,448]{1,0:T(8,128)S(1)} %copy-done.2), channel_id=1, replica_groups=mesh['row'=8,'col'=32] {'row'}, dimensions={0}, use_global_device_ids=true | all-gather | bytes 1032192 | tf_op jit(solution)/shard_map/all_gather | solution.py:18
  371.1 10.3 %convolution_subtract_fusion = f32[1792,448]{0,1:T(8,128)} fusion(f32[1792,448]{0,1:T(8,128)} %param.8, f32[1792,512]{1,0:T(8,128)} %copy-done.1, f32[512,448]{1,0:T(8,128)S(1)} %all_gather.11), kind=kOutput, calls=%fused_computation | convolution fusion | flops 4933304320 | bytes 11010048 | tf_op jit(solution)/shard_map/dot_general | solution.py:16
  381.5 8.5 %reduce-scatter.2.cloned.1.call-done = f32[64,448]{1,0:T(8,128)} async-done(((f32[512,448]{1,0:T(8,128)}), f32[64,448]{1,0:T(8,128)}) %reduce-scatter.2.cloned.1.call-update) | async-done | bytes 114704 | tf_op jit(solution)/shard_map/reduce_scatter | solution.py:29
Async XLA Ops:
  7.2 308.9 %copy-start = (f32[1792,448]{0,1:T(8,128)S(1)}, f32[1792,448]{0,1:T(8,128)}, u32[]{:S(2)}) copy-start(f32[1792,448]{0,1:T(8,128)} %param.9) | copy-start | bytes 9633796
  7.2 137.4 %all-gather.5.cloned.1.call-start = ((), (), s32[]{:S(2)}) async-start(), calls=%async_computation.2 | async-start | bytes 1081344 | tf_op jit(solution)/shard_map/all_gather | solution.py:9
  7.9 297.8 %all-gather.3.cloned.1.call-start = ((), (), s32[]{:S(2)}) async-start(), calls=%async_computation.1 | async-start | bytes 3784704 | tf_op jit(solution)/shard_map/all_gather | solution.py:11
  8.7 381.3 %reduce-scatter.2.cloned.1.call-start = ((), (), s32[]{:S(2)}) async-start(), calls=%async_computation.3 | async-start | bytes 1179648 | tf_op jit(solution)/shard_map/reduce_scatter | solution.py:29
  314.3 1.8 copy-start.1
  316.1 13.0 %copy-start.2 = (f32[64,448]{1,0:T(8,128)S(1)}, f32[64,448]{1,0:T(8,128)}, u32[]{:S(2)}) copy-start(f32[64,448]{1,0:T(8,128)} %param.7) | copy-start | bytes 344068
Sparse Core Ops, SparseCore 0:
  9.8 134.7 all-gather.4
  146.3 159.3 all-gather.2
  329.2 60.6 reduce-scatter.1
where the time goes:
time: 397 us; the launch traced here: 396 us
  waiting for transfers between devices  307 us (77%)
  blocking collectives  42 us (11%)
  matrix products  31.9 us (8%)
  between operations  13.8 us (3%)
    all_gather x1, waiting for transfers between devices, local(): lax.all_gather(panel_adj, 'col', axis=1, tiled=True)  161 us
    all_gather x1, waiting for transfers between devices, local(): inverse_all = lax.all_gather(inv_diag, 'col', axis=0, tiled=True)  136 us
    all_gather x1, blocking collectives, local(): lax.all_gather(row_panel, 'row', axis=0, tiled=True)  42 us
    dot_general x1, matrix products, local(): lax.dot_general(scaled, trailing_factor, (((0,), (0,)), ((), ())), precis...  13 us
    dot_general x1, matrix products, local(): jnp.dot(scaled, lax.all_gather(row_panel, 'row', axis=0, tiled=True), pre...  10.3 us
    dot_general x1, matrix products, local(): jnp.dot(lax.all_gather(panel_adj, 'col', axis=1, tiled=True), inverse_all...  8.55 us
    reduce_scatter x1, waiting for transfers between devices, local(): lax.psum_scatter(terms_local, 'row', scatter_dimension=0, tiled=True)  8.47 us
  transfers between devices with their start and end apart: 3, of which 3 were waited for; matrix products, arithmetic and copies ran while one was open for 3% of the time, Pallas kernels for 0%

commit v1 on v0

v1 whole, which is shorter than its diff:
```python
import jax
import jax.numpy as jnp
from jax import lax
from jax.experimental import pallas as pl
from jax.experimental.pallas import tpu as pltpu
from jax.sharding import PartitionSpec as P

MESH = pl.DeviceIdType.MESH
f32, bf16 = jnp.float32, jnp.bfloat16
ROWS, COLS, DEPTH, KS, HALF = 1792, 448, 512, 16, 256
WIDE = ROWS + HALF
STEPS = (0, 3, 1, 2)


def split(v):
    hi = v.astype(bf16)
    return hi, (v - hi.astype(f32)).astype(bf16)


def dot(a, b, dims):
    return lax.dot_general(a, b, (dims, ((), ())), preferred_element_type=f32)


def dot3(ah, al, bh, bl, dims):
    rows = ah.shape[0]
    both = dot(jnp.concatenate([ah, al], axis=0), bh, dims)
    return both[:rows] + both[rows:] + dot(ah, bl, dims)


def kernel(
    panel, inv, rowp, adj, fac, out, radj,
    z, fbuf, fh, fl, abuf, ph, pL, dbuf, ra, tm, tp, th, tl, wm, wp, wh, wl, us, ur,
    ssem, rsem, rs_s, rs_r, ts_s, ts_r, ws, us_s, us_r, loc, outsem,
):
    row, col = lax.axis_index("row"), lax.axis_index("col")
    h, core = row // 2, row % 2
    zl, x, y = col // 16, (col // 4) % 4, col % 4
    ia = x + core * (y - x)
    ib = y + core * (x - y)

    def device(zz, a, b):
        return (row, zz * 16 + a * (4 - 3 * core) + b * (1 + 3 * core))

    def off(i, d):
        return (i + d) % 4

    mate = device(1 - zl, ia, ib)
    ap, am = device(zl, off(ia, 1), ib), device(zl, off(ia, 3), ib)
    bp, bm = device(zl, ia, off(ib, 1)), device(zl, ia, off(ib, 3))
    partner = (2 * h + 1 - core, col)
    group = [(2 * ((h + d) % 4) + core, col) for d in (1, 2, 3)]

    def plane(dz):
        return zl if dz == 0 else 1 - zl

    own = z.at[zl, ia, ib]
    l_panel = pltpu.make_async_copy(panel, own.at[:, pl.ds(0, ROWS)], loc.at[0])
    l_inv = pltpu.make_async_copy(inv, dbuf, loc.at[1])
    l_row = pltpu.make_async_copy(rowp, ra.at[h], loc.at[2])
    l_fac = pltpu.make_async_copy(fac, fbuf, loc.at[3])
    l_adj = pltpu.make_async_copy(adj, abuf, loc.at[4])
    l_inv.start()
    l_panel.start()
    l_row.start()
    l_fac.start()
    l_adj.start()

    barrier = pltpu.get_barrier_semaphore()
    others = [mate, ap, am, bp, bm, partner] + group
    for other in others:
        pl.semaphore_signal(barrier, inc=1, device_id=other, device_id_type=MESH)
    l_inv.wait()
    d = dbuf[...]
    even = jnp.concatenate([d[:, 128 * i : 128 * i + 64] for i in range(4)], axis=1)
    odd = jnp.concatenate([d[:, 128 * i + 64 : 128 * i + 128] for i in range(4)], axis=1)
    z[zl, ia, ib, :, ROWS:WIDE] = jnp.where(core == 0, even, odd)
    l_panel.wait()
    l_row.wait()
    pl.semaphore_wait(barrier, len(others))

    sends = []

    def kind_a(dz, m):
        return 1 + dz * 4 + m

    def kind_b(dz, n, m):
        return 9 + (dz * 4 + n) * 4 + m

    def part(zz, a, b, half):
        ref = z.at[zz, a, b]
        return ref if half is None else ref.at[pl.ds(8 * half, 8)]

    def send(kind, ref, target):
        copy = pltpu.make_async_remote_copy(
            src_ref=ref, dst_ref=ref, send_sem=ssem.at[kind], recv_sem=rsem.at[kind],
            device_id=target, device_id_type=MESH,
        )
        copy.start()
        sends.append(copy)

    def arrive(kind, ref):
        pltpu.make_async_remote_copy(
            src_ref=ref, dst_ref=ref, send_sem=ssem.at[kind], recv_sem=rsem.at[kind],
            device_id=mate, device_id_type=MESH,
        ).wait_recv()

    def send_a(dz):
        ref = part(plane(dz), ia, ib, None)
        send(kind_a(dz, 0), ref, ap)
        send(kind_a(dz, 1), ref, am)

    def send_b(dz, n):
        ref = part(plane(dz), off(ia, STEPS[n]), ib, None)
        send(kind_b(dz, n, 0), ref, bp)
        send(kind_b(dz, n, 1), ref, bm)

    def relay_a(dz):
        for m, target in ((0, ap), (1, am)):
            a = off(ia, 3 if m == 0 else 1)
            arrive(kind_a(dz, m), part(plane(dz), a, ib, None))
            send(kind_a(dz, 2 + m), part(plane(dz), a, ib, m), target)
            send_b(dz, 1 + m)

    def relay_b(dz, n):
        a = off(ia, STEPS[n])
        for m, target in ((0, bp), (1, bm)):
            b = off(ib, 3 if m == 0 else 1)
            arrive(kind_b(dz, n, m), part(plane(dz), a, b, None))
            send(kind_b(dz, n, 2 + m), part(plane(dz), a, b, m), target)

    def far_a(dz):
        for m in (0, 1):
            arrive(kind_a(dz, 2 + m), part(plane(dz), off(ia, 2), ib, m))
        send_b(dz, 3)

    def far_b(dz, n):
        for m in (0, 1):
            arrive(kind_b(dz, n, 2 + m), part(plane(dz), off(ia, STEPS[n]), off(ib, 2), m))

    send(0, part(zl, ia, ib, None), mate)
    send_a(0)
    send_b(0, 0)
    r_sends = []
    for i in (1, 0, 2):
        copy = pltpu.make_async_remote_copy(
            src_ref=ra.at[h], dst_ref=ra.at[h], send_sem=rs_s.at[i], recv_sem=rs_r.at[i],
            device_id=group[i], device_id_type=MESH,
        )
        copy.start()
        r_sends.append(copy)

    l_fac.wait()
    for j in range(7):
        cut = pl.ds(256 * j, 256)
        hi, lo = split(fbuf[:, cut])
        fh[:, cut] = hi
        fl[:, cut] = lo

    t_sends = []

    def product(pieces):
        v = jnp.concatenate(
            [z[plane(dz), off(ia, STEPS[n]), :, :, 0:ROWS].reshape(64, ROWS) for dz, n in pieces], axis=0
        )
        hi, lo = split(v)
        for i, (dz, n) in enumerate(pieces):
            at = (plane(dz), off(ia, STEPS[n]))
            ph[at] = hi[64 * i : 64 * i + 64].reshape(4, 16, ROWS)
            pL[at] = lo[64 * i : 64 * i + 64].reshape(4, 16, ROWS)
        t = dot3(hi, lo, fh[...], fl[...], ((1,), (1,)))
        for i, (dz, n) in enumerate(pieces):
            at = (plane(dz), off(ia, STEPS[n]))
            tm[at] = t[64 * i : 64 * i + 64].reshape(4, 16, COLS)
        for dz, n in pieces:
            at = (plane(dz), off(ia, STEPS[n]))
            k = dz * 4 + n
            copy = pltpu.make_async_remote_copy(
                src_ref=tm.at[at], dst_ref=tp.at[at], send_sem=ts_s.at[k], recv_sem=ts_r.at[k],
                device_id=partner, device_id_type=MESH,
            )
            copy.start()
            t_sends.append(copy)

    arrive(0, part(1 - zl, ia, ib, None))
    send_a(1)
    send_b(1, 0)
    relay_a(0)
    relay_b(0, 0)
    relay_a(1)
    relay_b(1, 0)
    far_a(0)
    far_a(1)
    far_b(0, 0)
    far_b(1, 0)
    product([(0, 0), (1, 0)])
    relay_b(0, 1)
    relay_b(0, 2)
    relay_b(1, 1)
    relay_b(1, 2)
    far_b(0, 1)
    far_b(0, 2)
    product([(0, 1), (0, 2)])
    relay_b(0, 3)
    relay_b(1, 3)
    far_b(1, 1)
    far_b(1, 2)
    product([(1, 1), (1, 2)])
    far_b(0, 3)
    far_b(1, 3)
    product([(0, 3), (1, 3)])

    dh, dl = split(z[:, :, :, :, ROWS:WIDE].reshape(DEPTH, HALF))

    for dz in (0, 1):
        for n in range(4):
            k = dz * 4 + n
            ref = tp.at[plane(dz), off(ib, STEPS[n])]
            pltpu.make_async_remote_copy(
                src_ref=ref, dst_ref=ref, send_sem=ts_s.at[k], recv_sem=ts_r.at[k],
                device_id=partner, device_id_type=MESH,
            ).wait_recv()
    for zz in range(2):
        for i in range(4):
            for j in range(4):
                hi, lo = split(tm[zz, i, j] + tp[zz, j, i])
                th[zz, i, j] = hi
                tl[zz, i, j] = lo
    us[...] = dot3(
        dh.T, dl.T, th[...].reshape(DEPTH, COLS), tl[...].reshape(DEPTH, COLS), ((1,), (0,))
    ).reshape(4, 64, COLS)
    u_sends = []
    for i in (1, 0, 2):
        copy = pltpu.make_async_remote_copy(
            src_ref=us.at[(h + i + 1) % 4], dst_ref=ur.at[i], send_sem=us_s.at[i], recv_sem=us_r.at[i],
            device_id=group[i], device_id_type=MESH,
        )
        copy.start()
        u_sends.append(copy)

    for i in range(3):
        ref = ra.at[(h + 3 - i) % 4]
        pltpu.make_async_remote_copy(
            src_ref=ref, dst_ref=ref, send_sem=rs_s.at[i], recv_sem=rs_r.at[i],
            device_id=group[i], device_id_type=MESH,
        ).wait_recv()
    rh, rl = split(ra[...].reshape(HALF, COLS))
    wm[...] = dot3(dh, dl, rh, rl, ((1,), (0,))).reshape(2, 4, 4, 16, COLS)
    w_copy = pltpu.make_async_remote_copy(
        src_ref=wm, dst_ref=wp, send_sem=ws.at[0], recv_sem=ws.at[1], device_id=partner, device_id_type=MESH
    )
    w_copy.start()
    w_copy.wait_recv()
    for zz in range(2):
        for i in range(4):
            for j in range(4):
                hi, lo = split(wm[zz, i, j] + wp[zz, j, i])
                wh[zz, i, j] = hi
                wl[zz, i, j] = lo
    l_adj.wait()
    wth = wh[...].reshape(DEPTH, COLS).T
    wtl = wl[...].reshape(DEPTH, COLS).T
    outs = []
    for j in range(7):
        cut = pl.ds(256 * j, 256)
        pj = ph[:, :, :, :, cut].reshape(DEPTH, 256)
        qj = pL[:, :, :, :, cut].reshape(DEPTH, 256)
        abuf[:, cut] = abuf[:, cut] - dot3(wth, wtl, pj, qj, ((1,), (0,)))
        copy = pltpu.make_async_copy(abuf.at[:, cut], out.at[:, cut], outsem.at[j])
        copy.start()
        outs.append(copy)

    for i in range(3):
        pltpu.make_async_remote_copy(
            src_ref=ur.at[i], dst_ref=ur.at[i], send_sem=us_s.at[i], recv_sem=us_r.at[i],
            device_id=group[i], device_id_type=MESH,
        ).wait_recv()
    radj[...] = us[h] + ur[0] + ur[1] + ur[2]
    for copy in sends + r_sends + t_sends + u_sends + [w_copy]:
        copy.wait_send()
    for copy in outs:
        copy.wait()


def local(panel_adj, inv_diag, row_panel, trailing_adj, trailing_factor):
    dma = pltpu.SemaphoreType.DMA
    any_ = pl.BlockSpec(memory_space=pl.ANY)
    v = pltpu.VMEM
    out, radj = pl.pallas_call(
        kernel,
        out_shape=(
            jax.ShapeDtypeStruct((COLS, ROWS), f32),
            jax.ShapeDtypeStruct((64, COLS), f32),
        ),
        in_specs=[any_] * 5,
        out_specs=(any_, pl.BlockSpec(memory_space=pltpu.VMEM)),
        scratch_shapes=[
            v((2, 4, 4, KS, WIDE), f32),
            v((COLS, ROWS), f32),
            v((COLS, ROWS), bf16),
            v((COLS, ROWS), bf16),
            v((COLS, ROWS), f32),
            v((2, 4, 4, KS, ROWS), bf16),
            v((2, 4, 4, KS, ROWS), bf16),
            v((KS, DEPTH), f32),
            v((4, 64, COLS), f32),
            v((2, 4, 4, KS, COLS), f32),
            v((2, 4, 4, KS, COLS), f32),
            v((2, 4, 4, KS, COLS), bf16),
            v((2, 4, 4, KS, COLS), bf16),
            v((2, 4, 4, KS, COLS), f32),
            v((2, 4, 4, KS, COLS), f32),
            v((2, 4, 4, KS, COLS), bf16),
            v((2, 4, 4, KS, COLS), bf16),
            v((4, 64, COLS), f32),
            v((3, 64, COLS), f32),
            dma((41,)),
            dma((41,)),
            dma((3,)),
            dma((3,)),
            dma((8,)),
            dma((8,)),
            dma((2,)),
            dma((3,)),
            dma((3,)),
            dma((5,)),
            dma((7,)),
        ],
        compiler_params=pltpu.CompilerParams(
            collective_id=0, has_side_effects=True, vmem_limit_bytes=60 * 1024 * 1024
        ),
    )(panel_adj.T, inv_diag, row_panel, trailing_adj.T, trailing_factor.T)
    return out.T, radj


def solution(mesh):
    placed = (P("row", "col"), P("col", None), P("row", "col"), P("row", "col"), P("row", "col"))
    return jax.shard_map(
        local,
        mesh=mesh,
        in_specs=placed,
        out_specs=(P("row", "col"), P("row", "col")),
        check_vma=False,
    )
```

time: 397 us -> 65.6 us (0.17)
  waiting for transfers between devices: 307 us -> 0 us
  Pallas kernels: 0 us -> 60.3 us
  blocking collectives: 42 us -> 0 us
  matrix products: 31.9 us -> 0 us
  between operations: 13.8 us -> 0.65 us
    all_gather x2 -> x0, waiting for transfers between devices: 297 us -> none  [the longest x1 161 us: local(): lax.all_gather(panel_adj, 'col', axis=1, tiled=True)]
    pallas_call x0 -> x1, Pallas kernels: none -> 60.3 us  [local(): pl.pallas_call(kernel, out_shape=(jax.ShapeDtypeStruct((COLS, ROWS), f32)...]
    all_gather x1 -> x0, blocking collectives: 42 us -> none  [local(): lax.all_gather(row_panel, 'row', axis=0, tiled=True)]
    dot_general x3 -> x0, matrix products: 31.9 us -> none  [the longest x1 13 us: local(): lax.dot_general(scaled, trailing_factor, (((0,), (0,)), ((), ())), precis...]
    reduce_scatter x1 -> x0, waiting for transfers between devices: 8.47 us -> none  [local(): lax.psum_scatter(terms_local, 'row', scatter_dimension=0, tiled=True)]
  transfers between devices with their start and end apart: 3 -> 0, of which waited for: 3 -> 0; matrix products, arithmetic and copies ran while one was open for 3% -> 0% of each run, Pallas kernels for 0% -> 0%
where the time goes in v1:
time: 65.6 us; the launch traced here: 65.5 us
  Pallas kernels  60.3 us (92%)
  local copies, waits for them, and re-layouts  4.49 us (7%)
    pallas_call x1, Pallas kernels, local(): pl.pallas_call(kernel, out_shape=(jax.ShapeDtypeStruct((COLS, ROWS), f32)...  60.3 us
    unnamed x4, local copies, waits for them, and re-layouts  4.49 us

profile of v1, /device:TPU:1, one launch (start us, length us, event | category | flops | bytes accessed | tf_op | source)
XLA Modules:
  0.0 65.5 jit_solution(17005074135615434884)
XLA Ops:
  0.6 60.3 %shard_map.68 = (f32[448,1792]{1,0:T(8,128)}, f32[64,448]{1,0:T(8,128)}) custom-call(f32[16,1792]{1,0:T(8,128)} %bitcast.7, f32[16,512]{1,0:T(8,128)} %inv.1, f32[64,448]{1,0:T(8,128)} %rowp.1, f32[448,1792]{1,0:T(8,128)} %bitcast.4, f32[448,1792]{1,0:T(8,128)} %bitcast.5), custom_call_target="tpu_custom_call" | custom-call | tf_op jit(solution)/shard_map/pallas_call | solution.py:288
  61.0 0.0 copy-start
  61.0 3.8 %copy.9 = f32[1792,448]{0,1:T(8,128)} copy(f32[1792,448]{0,1:T(8,128)} %bitcast.6) | data formatting | bytes 6422528
  64.8 0.0 copy-done
  64.8 0.7 %copy.10 = f32[64,448]{1,0:T(8,128)} copy(f32[64,448]{1,0:T(8,128)S(1)} %copy-done) | data formatting | bytes 229376
Async XLA Ops:
  61.0 3.8 %copy-start = (f32[64,448]{1,0:T(8,128)S(1)}, f32[64,448]{1,0:T(8,128)}, u32[]{:S(2)}) copy-start(f32[64,448]{1,0:T(8,128)} %get-tuple-element.9) | copy-start | bytes 344068

commit v2 on v1

v2 whole, which is shorter than its diff:
```python
import jax
import jax.numpy as jnp
from jax import lax
from jax.experimental import pallas as pl
from jax.experimental.pallas import tpu as pltpu
from jax.sharding import PartitionSpec as P

MESH = pl.DeviceIdType.MESH
f32, bf16 = jnp.float32, jnp.bfloat16
ROWS, COLS, DEPTH, KS, HALF = 1792, 448, 512, 16, 256
WIDE = ROWS + HALF
STEPS = (0, 3, 1, 2)


def split(v):
    hi = v.astype(bf16)
    return hi, (v - hi.astype(f32)).astype(bf16)


def dot(a, b, dims):
    return lax.dot_general(a, b, (dims, ((), ())), preferred_element_type=f32)


def dot3(ah, al, bh, bl, dims):
    rows = ah.shape[0]
    both = dot(jnp.concatenate([ah, al], axis=0), bh, dims)
    return both[:rows] + both[rows:] + dot(ah, bl, dims)


def kernel(
    panel, inv, rowp, adj, fac, out, radj,
    z, fbuf, fh, fl, abuf, ph, pL, dbuf, ra, tm, tp, th, tl, wm, wp, wh, wl, us, ur,
    ssem, rsem, rs_s, rs_r, ts_s, ts_r, ws, us_s, us_r, loc,
):
    row, col = lax.axis_index("row"), lax.axis_index("col")
    h, core = row // 2, row % 2
    zl, x, y = col // 16, (col // 4) % 4, col % 4
    ia = x + core * (y - x)
    ib = y + core * (x - y)

    def device(zz, a, b):
        return (row, zz * 16 + a * (4 - 3 * core) + b * (1 + 3 * core))

    def off(i, d):
        return (i + d) % 4

    mate = device(1 - zl, ia, ib)
    ap, am = device(zl, off(ia, 1), ib), device(zl, off(ia, 3), ib)
    bp, bm = device(zl, ia, off(ib, 1)), device(zl, ia, off(ib, 3))
    partner = (2 * h + 1 - core, col)
    group = [(2 * ((h + d) % 4) + core, col) for d in (1, 3)]

    def plane(dz):
        return zl if dz == 0 else 1 - zl

    own = z.at[zl, ia, ib]
    l_panel = pltpu.make_async_copy(panel, own.at[:, pl.ds(0, ROWS)], loc.at[0])
    l_inv = pltpu.make_async_copy(inv, dbuf, loc.at[1])
    l_row = pltpu.make_async_copy(rowp, ra.at[h], loc.at[2])
    l_fac = pltpu.make_async_copy(fac, fbuf, loc.at[3])
    l_adj = pltpu.make_async_copy(adj, abuf, loc.at[4])
    l_inv.start()
    l_panel.start()
    l_row.start()
    l_fac.start()
    l_adj.start()

    barrier = pltpu.get_barrier_semaphore()
    others = [mate, ap, am, bp, bm, partner] + group
    for other in others:
        pl.semaphore_signal(barrier, inc=1, device_id=other, device_id_type=MESH)
    l_inv.wait()
    d = dbuf[...]
    even = jnp.concatenate([d[:, 128 * i : 128 * i + 64] for i in range(4)], axis=1)
    odd = jnp.concatenate([d[:, 128 * i + 64 : 128 * i + 128] for i in range(4)], axis=1)
    z[zl, ia, ib, :, ROWS:WIDE] = jnp.where(core == 0, even, odd)
    l_panel.wait()
    l_row.wait()
    pl.semaphore_wait(barrier, len(others))

    sends = []

    def kind_b(dz, n, m):
        return 8 + (dz * 4 + n) * 4 + m

    def part(zz, a, b, half):
        ref = z.at[zz, a, b]
        return ref if half is None else ref.at[pl.ds(8 * half, 8)]

    def send(kind, ref, target):
        copy = pltpu.make_async_remote_copy(
            src_ref=ref, dst_ref=ref, send_sem=ssem.at[kind], recv_sem=rsem.at[kind],
            device_id=target, device_id_type=MESH,
        )
        copy.start()
        sends.append(copy)

    def arrive(kind, ref):
        pltpu.make_async_remote_copy(
            src_ref=ref, dst_ref=ref, send_sem=ssem.at[kind], recv_sem=rsem.at[kind],
            device_id=mate, device_id_type=MESH,
        ).wait_recv()

    def line(dz, n):
        return part(plane(dz), off(ia, STEPS[n]), ib, None)

    def send_b(dz, n):
        send(kind_b(dz, n, 0), line(dz, n), bp)
        send(kind_b(dz, n, 1), line(dz, n), bm)

    def send_z(n):
        send(n, line(0, n), mate)

    def from_z(n):
        arrive(n, line(1, n))
        send_b(1, n)

    def relay_a(m):
        arrive(4 + m, line(0, 1 + m))
        send(6 + m, part(zl, off(ia, STEPS[1 + m]), ib, m), ap if m == 0 else am)
        send_b(0, 1 + m)
        send_z(1 + m)

    def relay_b(dz, n):
        a = off(ia, STEPS[n])
        for m, target in ((0, bp), (1, bm)):
            b = off(ib, STEPS[1 + m])
            arrive(kind_b(dz, n, m), part(plane(dz), a, b, None))
            send(kind_b(dz, n, 2 + m), part(plane(dz), a, b, m), target)

    def far_b(dz, n):
        for m in (0, 1):
            arrive(kind_b(dz, n, 2 + m), part(plane(dz), off(ia, STEPS[n]), off(ib, 2), m))

    hs = [off(h, d) for d in (0, 1, 2, 3)]
    nxt, prv = (2 * hs[1] + core, col), (2 * hs[3] + core, col)
    r_sends = []

    def r_copy(k, ref, target):
        return pltpu.make_async_remote_copy(
            src_ref=ref, dst_ref=ref, send_sem=rs_s.at[k], recv_sem=rs_r.at[k],
            device_id=target, device_id_type=MESH,
        )

    def r_send(k, ref, target):
        copy = r_copy(k, ref, target)
        copy.start()
        r_sends.append(copy)

    def r_own():
        r_send(0, ra.at[h], nxt)
        r_send(1, ra.at[h], prv)

    def r_relay():
        r_copy(0, ra.at[hs[3]], nxt).wait_recv()
        r_send(2, ra.at[hs[3], pl.ds(0, 32)], nxt)
        r_copy(1, ra.at[hs[1]], nxt).wait_recv()
        r_send(3, ra.at[hs[1], pl.ds(32, 32)], prv)

    def r_far():
        r_copy(2, ra.at[hs[2], pl.ds(0, 32)], nxt).wait_recv()
        r_copy(3, ra.at[hs[2], pl.ds(32, 32)], nxt).wait_recv()

    def split_factor():
        l_fac.wait()
        for j in range(7):
            cut = pl.ds(256 * j, 256)
            hi, lo = split(fbuf[:, cut])
            fh[:, cut] = hi
            fl[:, cut] = lo

    t_sends = []

    def product(pieces):
        at = [(plane(dz), off(ib, STEPS[m])) for dz, m in pieces]
        v = jnp.concatenate([z[zz, :, b, :, 0:ROWS].reshape(64, ROWS) for zz, b in at], axis=0)
        hi, lo = split(v)
        for i, (zz, b) in enumerate(at):
            ph[zz, :, b] = hi[64 * i : 64 * i + 64].reshape(4, 16, ROWS)
            pL[zz, :, b] = lo[64 * i : 64 * i + 64].reshape(4, 16, ROWS)
        t = dot3(hi, lo, fh[...], fl[...], ((1,), (1,)))
        for i, (zz, b) in enumerate(at):
            tm[zz, :, b] = t[64 * i : 64 * i + 64].reshape(4, 16, COLS)
        for (dz, m), (zz, b) in zip(pieces, at):
            k = dz * 4 + m
            copy = pltpu.make_async_remote_copy(
                src_ref=tm.at[zz, :, b], dst_ref=tp.at[zz, :, b], send_sem=ts_s.at[k], recv_sem=ts_r.at[k],
                device_id=partner, device_id_type=MESH,
            )
            copy.start()
            t_sends.append(copy)

    send_z(0)
    send(4, line(0, 0), ap)
    send(5, line(0, 0), am)
    send_b(0, 0)
    relay_a(0)
    relay_a(1)
    from_z(0)
    arrive(6, part(zl, off(ia, 2), ib, 0))
    arrive(7, part(zl, off(ia, 2), ib, 1))
    send_b(0, 3)
    send_z(3)
    r_own()
    relay_b(0, 0)
    from_z(1)
    from_z(2)
    relay_b(0, 1)
    relay_b(0, 2)
    from_z(3)
    relay_b(1, 0)
    split_factor()
    relay_b(0, 3)
    product([(0, 0), (1, 0)])
    relay_b(1, 1)
    relay_b(1, 2)
    product([(0, 1), (0, 2)])
    r_relay()
    relay_b(1, 3)
    product([(1, 1), (1, 2)])
    for n in range(4):
        far_b(0, n)
    for n in range(4):
        far_b(1, n)
    product([(0, 3), (1, 3)])

    dh, dl = split(z[:, :, :, :, ROWS:WIDE].reshape(DEPTH, HALF))

    for dz in (0, 1):
        for n in range(4):
            k = dz * 4 + n
            ref = tp.at[plane(dz), :, off(ia, STEPS[n])]
            pltpu.make_async_remote_copy(
                src_ref=ref, dst_ref=ref, send_sem=ts_s.at[k], recv_sem=ts_r.at[k],
                device_id=partner, device_id_type=MESH,
            ).wait_recv()
    for zz in range(2):
        for i in range(4):
            for j in range(4):
                hi, lo = split(tm[zz, i, j] + tp[zz, j, i])
                th[zz, i, j] = hi
                tl[zz, i, j] = lo
    us[...] = dot3(
        dh.T, dl.T, th[...].reshape(DEPTH, COLS), tl[...].reshape(DEPTH, COLS), ((1,), (0,))
    ).reshape(4, 64, COLS)
    u_sends = []

    def u_copy(k, src, target):
        return pltpu.make_async_remote_copy(
            src_ref=src, dst_ref=ur.at[k], send_sem=us_s.at[k], recv_sem=us_r.at[k],
            device_id=target, device_id_type=MESH,
        )

    def u_send(k, block, half, target):
        copy = u_copy(k, us.at[block, pl.ds(32 * half, 32)], target)
        copy.start()
        u_sends.append(copy)

    def u_arrive(k):
        u_copy(k, us.at[h, pl.ds(0, 32)], nxt).wait_recv()

    u_send(0, hs[2], 0, nxt)
    u_send(1, hs[2], 1, prv)
    u_send(2, hs[1], 1, nxt)
    u_send(3, hs[3], 0, prv)

    r_far()
    rh, rl = split(ra[...].reshape(HALF, COLS))
    wm[...] = dot3(dh, dl, rh, rl, ((1,), (0,))).reshape(2, 4, 4, 16, COLS)
    w_copy = pltpu.make_async_remote_copy(
        src_ref=wm, dst_ref=wp, send_sem=ws.at[0], recv_sem=ws.at[1], device_id=partner, device_id_type=MESH
    )
    w_copy.start()
    w_copy.wait_recv()
    for zz in range(2):
        for i in range(4):
            for j in range(4):
                hi, lo = split(wm[zz, i, j] + wp[zz, j, i])
                wh[zz, i, j] = hi
                wl[zz, i, j] = lo
    u_arrive(0)
    us[hs[1], 0:32] += ur[0]
    u_send(4, hs[1], 0, nxt)
    u_arrive(1)
    us[hs[3], 32:64] += ur[1]
    u_send(5, hs[3], 1, prv)
    l_adj.wait()
    wth = wh[...].reshape(DEPTH, COLS).T
    wtl = wl[...].reshape(DEPTH, COLS).T
    for j in range(7):
        cut = pl.ds(256 * j, 256)
        pj = ph[:, :, :, :, cut].reshape(DEPTH, 256)
        qj = pL[:, :, :, :, cut].reshape(DEPTH, 256)
        out[:, cut] = abuf[:, cut] - dot3(wth, wtl, pj, qj, ((1,), (0,)))

    for k in (2, 3, 4, 5):
        u_arrive(k)
    radj[0:32] = us[h, 0:32] + ur[4] + ur[3]
    radj[32:64] = us[h, 32:64] + ur[2] + ur[5]
    for copy in sends + r_sends + t_sends + u_sends + [w_copy]:
        copy.wait_send()


def local(panel_adj, inv_diag, row_panel, trailing_adj, trailing_factor):
    dma = pltpu.SemaphoreType.DMA
    hbm = pl.BlockSpec(memory_space=pltpu.HBM)
    v = pltpu.VMEM
    out, radj = pl.pallas_call(
        kernel,
        out_shape=(
            v((COLS, ROWS), f32),
            v((64, COLS), f32),
        ),
        in_specs=[hbm] * 5,
        out_specs=(pl.BlockSpec(memory_space=pltpu.VMEM),) * 2,
        scratch_shapes=[
            v((2, 4, 4, KS, WIDE), f32),
            v((COLS, ROWS), f32),
            v((COLS, ROWS), bf16),
            v((COLS, ROWS), bf16),
            v((COLS, ROWS), f32),
            v((2, 4, 4, KS, ROWS), bf16),
            v((2, 4, 4, KS, ROWS), bf16),
            v((KS, DEPTH), f32),
            v((4, 64, COLS), f32),
            v((2, 4, 4, KS, COLS), f32),
            v((2, 4, 4, KS, COLS), f32),
            v((2, 4, 4, KS, COLS), bf16),
            v((2, 4, 4, KS, COLS), bf16),
            v((2, 4, 4, KS, COLS), f32),
            v((2, 4, 4, KS, COLS), f32),
            v((2, 4, 4, KS, COLS), bf16),
            v((2, 4, 4, KS, COLS), bf16),
            v((4, 64, COLS), f32),
            v((6, 32, COLS), f32),
            dma((40,)),
            dma((40,)),
            dma((4,)),
            dma((4,)),
            dma((8,)),
            dma((8,)),
            dma((2,)),
            dma((6,)),
            dma((6,)),
            dma((5,)),
        ],
        compiler_params=pltpu.CompilerParams(
            collective_id=0, has_side_effects=True, vmem_limit_bytes=63_500_000
        ),
    )(panel_adj.T, inv_diag, row_panel, trailing_adj.T, trailing_factor.T)
    return out.T, radj


def solution(mesh):
    placed = (P("row", "col"), P("col", None), P("row", "col"), P("row", "col"), P("row", "col"))
    return jax.shard_map(
        local,
        mesh=mesh,
        in_specs=placed,
        out_specs=(P("row", "col"), P("row", "col")),
        check_vma=False,
    )
```

time: 65.6 us -> 54 us (0.82)
  Pallas kernels: 60.3 us -> 50.9 us
  local copies, waits for them, and re-layouts: 4.49 us -> 2.34 us
    pallas_call x1, Pallas kernels: 60.3 us -> 50.9 us  [local(): pl.pallas_call(kernel, out_shape=(v((COLS, ROWS), f32), v((64, COLS), f32...]
    unnamed x4 -> x2, local copies, waits for them, and re-layouts: 4.49 us -> 2.34 us
where the time goes in v2:
time: 54 us; the launch traced here: 53.9 us
  Pallas kernels  50.9 us (94%)
  local copies, waits for them, and re-layouts  2.34 us (4%)
  between operations  0.64 us (1%)
    pallas_call x1, Pallas kernels, local(): pl.pallas_call(kernel, out_shape=(v((COLS, ROWS), f32), v((64, COLS), f32...  50.9 us
    unnamed x2, local copies, waits for them, and re-layouts  2.34 us

profile of v2, /device:TPU:1, one launch (start us, length us, event | category | flops | bytes accessed | tf_op | source)
XLA Modules:
  0.0 53.9 jit_solution(16687809187879386344)
XLA Ops:
  0.6 50.9 %shard_map.68 = (f32[448,1792]{1,0:T(8,128)S(1)}, f32[64,448]{1,0:T(8,128)S(1)}) custom-call(f32[16,1792]{1,0:T(8,128)} %bitcast.7, f32[16,512]{1,0:T(8,128)} %inv.1, f32[64,448]{1,0:T(8,128)} %rowp.1, f32[448,1792]{1,0:T(8,128)} %bitcast.5, f32[448,1792]{1,0:T(8,128)} %bitcast.6), custom_call_target="tpu_custom_call" | custom-call | tf_op jit(solution)/shard_map/pallas_call | solution.py:308
  51.5 1.7 %copy.9 = f32[1792,448]{0,1:T(8,128)} copy(f32[1792,448]{0,1:T(8,128)S(1)} %bitcast.4) | data formatting | bytes 6422528
  53.2 0.7 %copy.10 = f32[64,448]{1,0:T(8,128)} copy(f32[64,448]{1,0:T(8,128)S(1)} %get-tuple-element.7) | data formatting | bytes 229376

commit v3 on v2

--- a/solution.py
+++ b/solution.py
@@ -59,29 +59,25 @@
     l_row = pltpu.make_async_copy(rowp, ra.at[h], loc.at[2])
     l_fac = pltpu.make_async_copy(fac, fbuf, loc.at[3])
     l_adj = pltpu.make_async_copy(adj, abuf, loc.at[4])
-    l_inv.start()
-    l_panel.start()
-    l_row.start()
-    l_fac.start()
-    l_adj.start()
-
     barrier = pltpu.get_barrier_semaphore()
     others = [mate, ap, am, bp, bm, partner] + group
     for other in others:
         pl.semaphore_signal(barrier, inc=1, device_id=other, device_id_type=MESH)
+    l_inv.start()
+    l_panel.start()
+    l_row.start()
     l_inv.wait()
     d = dbuf[...]
     even = jnp.concatenate([d[:, 128 * i : 128 * i + 64] for i in range(4)], axis=1)
     odd = jnp.concatenate([d[:, 128 * i + 64 : 128 * i + 128] for i in range(4)], axis=1)
     z[zl, ia, ib, :, ROWS:WIDE] = jnp.where(core == 0, even, odd)
     l_panel.wait()
-    l_row.wait()
     pl.semaphore_wait(barrier, len(others))
 
     sends = []
 
     def kind_b(dz, n, m):
-        return 8 + (dz * 4 + n) * 4 + m
+        return 11 + (dz * 4 + n) * 4 + m
 
     def part(zz, a, b, half):
         ref = z.at[zz, a, b]
@@ -94,6 +90,7 @@
         )
         copy.start()
         sends.append(copy)
+        return copy
 
     def arrive(kind, ref):
         pltpu.make_async_remote_copy(
@@ -108,18 +105,39 @@
         send(kind_b(dz, n, 0), line(dz, n), bp)
         send(kind_b(dz, n, 1), line(dz, n), bm)
 
-    def send_z(n):
-        send(n, line(0, n), mate)
-
-    def from_z(n):
-        arrive(n, line(1, n))
-        send_b(1, n)
+    def half(dz, m):
+        return part(plane(dz), off(ia, STEPS[1 + m]), ib, m)
+
+    def other_half(dz, m):
+        return part(plane(dz), off(ia, STEPS[1 + m]), ib, 1 - m)
+
+    def onward(m):
+        return ap if m == 0 else am
 
     def relay_a(m):
-        arrive(4 + m, line(0, 1 + m))
-        send(6 + m, part(zl, off(ia, STEPS[1 + m]), ib, m), ap if m == 0 else am)
+        arrive(3 + m, line(0, 1 + m))
+        send(5 + m, half(0, m), onward(m))
+        send(1 + m, other_half(0, m), mate)
         send_b(0, 1 + m)
-        send_z(1 + m)
+
+    def from_mate():
+        arrive(0, line(1, 0))
+        for m in (0, 1):
+            send(7 + m, part(1 - zl, ia, ib, m), onward(m))
+        send_b(1, 0)
+
+    def relay_mate(m):
+        arrive(7 + m, half(1, m))
+        send(9 + m, half(1, m), onward(m))
+
+    def from_z(m):
+        arrive(1 + m, other_half(1, m))
+        send_b(1, 1 + m)
+
+    def far_a(dz):
+        for m in (0, 1):
+            arrive((5 if dz == 0 else 9) + m, part(plane(dz), off(ia, 2), ib, m))
+        send_b(dz, 3)
 
     def relay_b(dz, n):
         a = off(ia, STEPS[n])
@@ -148,6 +166,7 @@
         r_sends.append(copy)
 
     def r_own():
+        l_row.wait()
         r_send(0, ra.at[h], nxt)
         r_send(1, ra.at[h], prv)
 
@@ -190,56 +209,73 @@
             copy.start()
             t_sends.append(copy)
 
-    send_z(0)
-    send(4, line(0, 0), ap)
-    send(5, line(0, 0), am)
+    def t_wait(dz, m):
+        ref = tp.at[plane(dz), :, off(ia, STEPS[m])]
+        k = dz * 4 + m
+        pltpu.make_async_remote_copy(
+            src_ref=ref, dst_ref=ref, send_sem=ts_s.at[k], recv_sem=ts_r.at[k],
+            device_id=partner, device_id_type=MESH,
+        ).wait_recv()
+
+    def t_sum(n, m):
+        a, b = off(ia, STEPS[n]), off(ib, STEPS[m])
+        for zz in range(2):
+            hi, lo = split(tm[zz, a, b] + tp[zz, b, a])
+            th[zz, a, b] = hi
+            tl[zz, a, b] = lo
+
+    first = send(3, line(0, 0), ap)
+    send(4, line(0, 0), am)
+    send(0, line(0, 0), mate)
+    l_fac.start()
+    l_adj.start()
+    first.wait_send()
+    del sends[0]
     send_b(0, 0)
     relay_a(0)
     relay_a(1)
-    from_z(0)
-    arrive(6, part(zl, off(ia, 2), ib, 0))
-    arrive(7, part(zl, off(ia, 2), ib, 1))
-    send_b(0, 3)
-    send_z(3)
+    from_mate()
     r_own()
     relay_b(0, 0)
+    split_factor()
+    relay_mate(0)
+    relay_mate(1)
+    far_a(0)
+    from_z(0)
     from_z(1)
-    from_z(2)
     relay_b(0, 1)
     relay_b(0, 2)
-    from_z(3)
+    far_a(1)
     relay_b(1, 0)
-    split_factor()
     relay_b(0, 3)
-    product([(0, 0), (1, 0)])
+    product([(0, 0), (0, 1)])
     relay_b(1, 1)
     relay_b(1, 2)
-    product([(0, 1), (0, 2)])
+    product([(0, 2), (1, 0)])
     r_relay()
     relay_b(1, 3)
     product([(1, 1), (1, 2)])
     for n in range(4):
         far_b(0, n)
+    product([(0, 3)])
+    for dz in (0, 1):
+        for m in (0, 1, 2):
+            t_wait(dz, m)
+    for n in (0, 1, 2):
+        for m in (0, 1, 2):
+            t_sum(n, m)
     for n in range(4):
         far_b(1, n)
-    product([(0, 3), (1, 3)])
+    product([(1, 3)])
 
     dh, dl = split(z[:, :, :, :, ROWS:WIDE].reshape(DEPTH, HALF))
 
-    for dz in (0, 1):
-        for n in range(4):
-            k = dz * 4 + n
-            ref = tp.at[plane(dz), :, off(ia, STEPS[n])]
-            pltpu.make_async_remote_copy(
-                src_ref=ref, dst_ref=ref, send_sem=ts_s.at[k], recv_sem=ts_r.at[k],
-                device_id=partner, device_id_type=MESH,
-            ).wait_recv()
-    for zz in range(2):
-        for i in range(4):
-            for j in range(4):
-                hi, lo = split(tm[zz, i, j] + tp[zz, j, i])
-                th[zz, i, j] = hi
-                tl[zz, i, j] = lo
+    t_wait(0, 3)
+    t_wait(1, 3)
+    for n in range(4):
+        for m in range(4):
+            if n == 3 or m == 3:
+                t_sum(n, m)
     us[...] = dot3(
         dh.T, dl.T, th[...].reshape(DEPTH, COLS), tl[...].reshape(DEPTH, COLS), ((1,), (0,))
     ).reshape(4, 64, COLS)
@@ -271,6 +307,12 @@
         src_ref=wm, dst_ref=wp, send_sem=ws.at[0], recv_sem=ws.at[1], device_id=partner, device_id_type=MESH
     )
     w_copy.start()
+    u_arrive(0)
+    us[hs[1], 0:32] += ur[0]
+    u_send(4, hs[1], 0, nxt)
+    u_arrive(1)
+    us[hs[3], 32:64] += ur[1]
+    u_send(5, hs[3], 1, prv)
     w_copy.wait_recv()
     for zz in range(2):
         for i in range(4):
@@ -278,12 +320,6 @@
                 hi, lo = split(wm[zz, i, j] + wp[zz, j, i])
                 wh[zz, i, j] = hi
                 wl[zz, i, j] = lo
-    u_arrive(0)
-    us[hs[1], 0:32] += ur[0]
-    u_send(4, hs[1], 0, nxt)
-    u_arrive(1)
-    us[hs[3], 32:64] += ur[1]
-    u_send(5, hs[3], 1, prv)
     l_adj.wait()
     wth = wh[...].reshape(DEPTH, COLS).T
     wtl = wl[...].reshape(DEPTH, COLS).T
@@ -299,6 +335,17 @@
     radj[32:64] = us[h, 32:64] + ur[2] + ur[5]
     for copy in sends + r_sends + t_sends + u_sends + [w_copy]:
         copy.wait_send()
+
+
+def finish(a, b, out_a, out_b, sem):
+    copies = [pltpu.make_async_copy(b, out_b, sem.at[7])]
+    for j in range(7):
+        cut = pl.ds(64 * j, 64)
+        copies.append(pltpu.make_async_copy(a.at[cut], out_a.at[cut], sem.at[j]))
+    for copy in copies:
+        copy.start()
+    for copy in copies:
+        copy.wait()
 
 
 def local(panel_adj, inv_diag, row_panel, trailing_adj, trailing_factor):
@@ -333,8 +380,8 @@
             v((2, 4, 4, KS, COLS), bf16),
             v((4, 64, COLS), f32),
             v((6, 32, COLS), f32),
-            dma((40,)),
-            dma((40,)),
+            dma((43,)),
+            dma((43,)),
             dma((4,)),
             dma((4,)),
             dma((8,)),
@@ -348,6 +395,17 @@
             collective_id=0, has_side_effects=True, vmem_limit_bytes=63_500_000
         ),
     )(panel_adj.T, inv_diag, row_panel, trailing_adj.T, trailing_factor.T)
+    out, radj = pl.pallas_call(
+        finish,
+        out_shape=(
+            jax.ShapeDtypeStruct((COLS, ROWS), f32),
+            jax.ShapeDtypeStruct((64, COLS), f32),
+        ),
+        in_specs=[pl.BlockSpec(memory_space=pl.ANY)] * 2,
+        out_specs=(hbm,) * 2,
+        scratch_shapes=[dma((8,))],
+        compiler_params=pltpu.CompilerParams(vmem_limit_bytes=1024 * 1024),
+    )(out, radj)
     return out.T, radj
 
 

time: 54 us -> 51.6 us (0.956)
  local copies, waits for them, and re-layouts: 2.34 us -> 0 us
    unnamed x2 -> x0, local copies, waits for them, and re-layouts: 2.34 us -> none
    pallas_call x1, Pallas kernels: 50.9 us -> 49.1 us  [local(): pl.pallas_call(kernel, out_shape=(v((COLS, ROWS), f32), v((64, COLS), f32...]
    pallas_call x0 -> x1, Pallas kernels: none -> 1.79 us  [local(): pl.pallas_call(finish, out_shape=(jax.ShapeDtypeStruct((COLS, ROWS), f32)...]
where the time goes in v3:
time: 51.6 us; the launch traced here: 51.5 us
  Pallas kernels  50.9 us (99%)
  between operations  0.64 us (1%)
    pallas_call x1, Pallas kernels, local(): pl.pallas_call(kernel, out_shape=(v((COLS, ROWS), f32), v((64, COLS), f32...  49.1 us
    pallas_call x1, Pallas kernels, local(): pl.pallas_call(finish, out_shape=(jax.ShapeDtypeStruct((COLS, ROWS), f32)...  1.79 us

profile of v3, /device:TPU:1, one launch (start us, length us, event | category | flops | bytes accessed | tf_op | source)
XLA Modules:
  0.0 51.5 jit_solution(2158744452878175707)
XLA Ops:
  0.6 49.1 %shard_map.68 = (f32[448,1792]{1,0:T(8,128)S(1)}, f32[64,448]{1,0:T(8,128)S(1)}) custom-call(f32[16,1792]{1,0:T(8,128)} %bitcast.6, f32[16,512]{1,0:T(8,128)} %inv.1, f32[64,448]{1,0:T(8,128)} %rowp.1, f32[448,1792]{1,0:T(8,128)} %bitcast.4, f32[448,1792]{1,0:T(8,128)} %bitcast.5), custom_call_target="tpu_custom_call" | custom-call | tf_op jit(solution)/shard_map/pallas_call | solution.py:355
  49.7 1.8 %shard_map.69 = (f32[448,1792]{1,0:T(8,128)}, f32[64,448]{1,0:T(8,128)}) custom-call(f32[448,1792]{1,0:T(8,128)S(1)} %get-tuple-element.6.a, f32[64,448]{1,0:T(8,128)S(1)} %get-tuple-element.7.b), custom_call_target="tpu_custom_call" | custom-call | tf_op jit(solution)/shard_map/pallas_call | solution.py:398

commit v4 on v3

--- a/solution.py
+++ b/solution.py
@@ -81,7 +81,12 @@
 
     def part(zz, a, b, half):
         ref = z.at[zz, a, b]
-        return ref if half is None else ref.at[pl.ds(8 * half, 8)]
+        return ref if half is None else ref.at[pl.ds(8 * half if isinstance(half, int) else pl.multiple_of(8 * half, 8), 8)]
+
+    wa, wb = 1 - jnp.minimum(ia, 1), 1 - jnp.minimum(ib, 1)
+
+    def side(plus, minus, m):
+        return tuple(p + m * (q - p) for p, q in zip(plus, minus))
 
     def send(kind, ref, target):
         copy = pltpu.make_async_remote_copy(
@@ -105,20 +110,27 @@
         send(kind_b(dz, n, 0), line(dz, n), bp)
         send(kind_b(dz, n, 1), line(dz, n), bm)
 
+    def beside(dz, m):
+        return part(plane(dz), off(ia, 3 - 2 * m), ib, None)
+
     def half(dz, m):
-        return part(plane(dz), off(ia, STEPS[1 + m]), ib, m)
+        return part(plane(dz), off(ia, 3 - 2 * m), ib, m)
 
     def other_half(dz, m):
-        return part(plane(dz), off(ia, STEPS[1 + m]), ib, 1 - m)
+        return part(plane(dz), off(ia, 3 - 2 * m), ib, 1 - m)
 
     def onward(m):
-        return ap if m == 0 else am
+        return side(ap, am, m)
+
+    def send_beside(dz, m):
+        send(kind_b(dz, 1 + m, 0), beside(dz, m), bp)
+        send(kind_b(dz, 1 + m, 1), beside(dz, m), bm)
 
     def relay_a(m):
-        arrive(3 + m, line(0, 1 + m))
+        arrive(3 + m, beside(0, m))
         send(5 + m, half(0, m), onward(m))
         send(1 + m, other_half(0, m), mate)
-        send_b(0, 1 + m)
+        send_beside(0, m)
 
     def from_mate():
         arrive(0, line(1, 0))
@@ -132,7 +144,7 @@
 
     def from_z(m):
         arrive(1 + m, other_half(1, m))
-        send_b(1, 1 + m)
+        send_beside(1, m)
 
     def far_a(dz):
         for m in (0, 1):
@@ -141,10 +153,10 @@
 
     def relay_b(dz, n):
         a = off(ia, STEPS[n])
-        for m, target in ((0, bp), (1, bm)):
-            b = off(ib, STEPS[1 + m])
+        for m in (wb, 1 - wb):
+            b = off(ib, 3 - 2 * m)
             arrive(kind_b(dz, n, m), part(plane(dz), a, b, None))
-            send(kind_b(dz, n, 2 + m), part(plane(dz), a, b, m), target)
+            send(kind_b(dz, n, 2 + m), part(plane(dz), a, b, m), side(bp, bm, m))
 
     def far_b(dz, n):
         for m in (0, 1):
@@ -232,14 +244,14 @@
     first.wait_send()
     del sends[0]
     send_b(0, 0)
-    relay_a(0)
-    relay_a(1)
+    relay_a(wa)
+    relay_a(1 - wa)
     from_mate()
     r_own()
     relay_b(0, 0)
     split_factor()
-    relay_mate(0)
-    relay_mate(1)
+    relay_mate(wa)
+    relay_mate(1 - wa)
     far_a(0)
     from_z(0)
     from_z(1)

time: 51.6 us -> 50.9 us (0.986)
  Pallas kernels: 50.9 us -> 50.1 us
    pallas_call x1, Pallas kernels: 49.1 us -> 48.3 us  [local(): pl.pallas_call(kernel, out_shape=(v((COLS, ROWS), f32), v((64, COLS), f32...]
where the time goes in v4:
time: 50.9 us; the launch traced here: 50.8 us
  Pallas kernels  50.1 us (98%)
  between operations  0.64 us (1%)
    pallas_call x1, Pallas kernels, local(): pl.pallas_call(kernel, out_shape=(v((COLS, ROWS), f32), v((64, COLS), f32...  48.3 us
    pallas_call x1, Pallas kernels, local(): pl.pallas_call(finish, out_shape=(jax.ShapeDtypeStruct((COLS, ROWS), f32)...  1.79 us

profile of v4, /device:TPU:1, one launch (start us, length us, event | category | flops | bytes accessed | tf_op | source)
XLA Modules:
  0.0 50.8 jit_solution(17269842581264291313)
XLA Ops:
  0.6 48.3 %shard_map.68 = (f32[448,1792]{1,0:T(8,128)S(1)}, f32[64,448]{1,0:T(8,128)S(1)}) custom-call(f32[16,1792]{1,0:T(8,128)} %bitcast.6, f32[16,512]{1,0:T(8,128)} %inv.1, f32[64,448]{1,0:T(8,128)} %rowp.1, f32[448,1792]{1,0:T(8,128)} %bitcast.4, f32[448,1792]{1,0:T(8,128)} %bitcast.5), custom_call_target="tpu_custom_call" | custom-call | tf_op jit(solution)/shard_map/pallas_call | solution.py:367
  49.0 1.8 %shard_map.69 = (f32[448,1792]{1,0:T(8,128)}, f32[64,448]{1,0:T(8,128)}) custom-call(f32[448,1792]{1,0:T(8,128)S(1)} %get-tuple-element.6.a, f32[64,448]{1,0:T(8,128)S(1)} %get-tuple-element.7.b), custom_call_target="tpu_custom_call" | custom-call | tf_op jit(solution)/shard_map/pallas_call | solution.py:410

commit v5 on v4

--- a/solution.py
+++ b/solution.py
@@ -29,7 +29,7 @@
 
 def kernel(
     panel, inv, rowp, adj, fac, out, radj,
-    z, fbuf, fh, fl, abuf, ph, pL, dbuf, ra, tm, tp, th, tl, wm, wp, wh, wl, us, ur,
+    z, fbuf, fh, fl, abuf, ph, pL, dbuf, ra, tm, tp, th, tl, dth, dtl, wm, wp, wh, wl, us, ur,
     ssem, rsem, rs_s, rs_r, ts_s, ts_r, ws, us_s, us_r, loc,
 ):
     row, col = lax.axis_index("row"), lax.axis_index("col")
@@ -281,6 +281,8 @@
     product([(1, 3)])
 
     dh, dl = split(z[:, :, :, :, ROWS:WIDE].reshape(DEPTH, HALF))
+    dth[...] = dh.T
+    dtl[...] = dl.T
 
     t_wait(0, 3)
     t_wait(1, 3)
@@ -289,7 +291,7 @@
             if n == 3 or m == 3:
                 t_sum(n, m)
     us[...] = dot3(
-        dh.T, dl.T, th[...].reshape(DEPTH, COLS), tl[...].reshape(DEPTH, COLS), ((1,), (0,))
+        dth[...], dtl[...], th[...].reshape(DEPTH, COLS), tl[...].reshape(DEPTH, COLS), ((1,), (0,))
     ).reshape(4, 64, COLS)
     u_sends = []
 
@@ -386,6 +388,8 @@
             v((2, 4, 4, KS, COLS), f32),
             v((2, 4, 4, KS, COLS), bf16),
             v((2, 4, 4, KS, COLS), bf16),
+            v((HALF, DEPTH), bf16),
+            v((HALF, DEPTH), bf16),
             v((2, 4, 4, KS, COLS), f32),
             v((2, 4, 4, KS, COLS), f32),
             v((2, 4, 4, KS, COLS), bf16),

time: 50.9 us -> 51.5 us (1.012)
  Pallas kernels: 50.1 us -> 50.8 us
    pallas_call x1, Pallas kernels: 48.3 us -> 49 us  [local(): pl.pallas_call(kernel, out_shape=(v((COLS, ROWS), f32), v((64, COLS), f32...]
where the time goes in v5:
time: 51.5 us; the launch traced here: 51.4 us
  Pallas kernels  50.8 us (99%)
  between operations  0.64 us (1%)
    pallas_call x1, Pallas kernels, local(): pl.pallas_call(kernel, out_shape=(v((COLS, ROWS), f32), v((64, COLS), f32...  49 us
    pallas_call x1, Pallas kernels, local(): pl.pallas_call(finish, out_shape=(jax.ShapeDtypeStruct((COLS, ROWS), f32)...  1.79 us

profile of v5, /device:TPU:1, one launch (start us, length us, event | category | flops | bytes accessed | tf_op | source)
XLA Modules:
  0.0 51.4 jit_solution(8592605750022938186)
XLA Ops:
  0.6 49.0 %shard_map.68 = (f32[448,1792]{1,0:T(8,128)S(1)}, f32[64,448]{1,0:T(8,128)S(1)}) custom-call(f32[16,1792]{1,0:T(8,128)} %bitcast.6, f32[16,512]{1,0:T(8,128)} %inv.1, f32[64,448]{1,0:T(8,128)} %rowp.1, f32[448,1792]{1,0:T(8,128)} %bitcast.4, f32[448,1792]{1,0:T(8,128)} %bitcast.5), custom_call_target="tpu_custom_call" | custom-call | tf_op jit(solution)/shard_map/pallas_call | solution.py:369
  49.6 1.8 %shard_map.69 = (f32[448,1792]{1,0:T(8,128)}, f32[64,448]{1,0:T(8,128)}) custom-call(f32[448,1792]{1,0:T(8,128)S(1)} %get-tuple-element.6.a, f32[64,448]{1,0:T(8,128)S(1)} %get-tuple-element.7.b), custom_call_target="tpu_custom_call" | custom-call | tf_op jit(solution)/shard_map/pallas_call | solution.py:414
